TPU v7x, 32 devices: a whole 2x2x4 slice. The times are simulated.
32 devices in a mesh: req: 4 (over x, core), mlp: 8 (over z, y).
Axes of the slice: x: 2, y: 2, z: 4, core: 2. Of those that a mesh axis runs over, the one named last changes fastest.
Arguments:
- resid: bfloat16 [4096, 3072], P(('req', 'mlp')), may hold values from -6 to 6
- queries: bfloat16 [4096, 1536], P(('req', 'mlp')), may hold values from -240 to 240
- fresh_keys: bfloat16 [4096, 256], P(('req', 'mlp')), may hold values from -6 to 6
- fresh_values: bfloat16 [4096, 256], P(('req', 'mlp')), may hold values from -6 to 6
- paged_key_cache: bfloat16 [64, 128, 256], P(('req', 'mlp')), may hold values from -6 to 6
- paged_value_cache: bfloat16 [64, 128, 256], P(('req', 'mlp')), may hold values from -6 to 6
- page_table: int32 [4, 16], P('req'), may hold values from 0 to 15, as said below
- cache_lengths: int32 [4], P('req'), may hold values from 1 to 2048, as said below
- out_weight: bfloat16 [1536, 3072], replicated, may hold values from -0.15625 to 0.15625
- norm_gain: float32 [3072], replicated, may hold values from 0.5 to 1.5
- gate_weight: bfloat16 [3072, 8192], P('req', 'mlp'), may hold values from -0.109375 to 0.109375
- up_weight: bfloat16 [3072, 8192], P('req', 'mlp'), may hold values from -0.109375 to 0.109375
- down_weight: bfloat16 [8192, 3072], P('mlp', 'req'), may hold values from -0.0625 to 0.0625
Outputs:
- layer_out: bfloat16 [4096, 3072], P(('req', 'mlp'))
Inputs may be any that keep to these rules, and one draw needn't show every extreme that they name: `page_table`: within the 1 request of one index of req the entries are a permutation of 0 to 15. `cache_lengths`: half of the requests hold at most 128 cached tokens, the other half more than 1920; some request holds exactly 2048.
All inputs are finite; a program needn't handle non-finite values.
Results may differ from a plain program's by a relative error of at most 0.0085.
Values may be sent and summed in bfloat16 or wider, within the bound.
A program may use at most 128 MiB of HBM per device.

v0:
```python
import jax
import jax.numpy as jnp
from jax import lax
from jax.sharding import PartitionSpec as P

QUERY_HEADS = 12
KEY_VALUE_HEADS = 2
HEAD_SIZE = 128
REQ_DEV = 1


def body(
    resid,
    queries,
    fresh_keys,
    fresh_values,
    paged_key_cache,
    paged_value_cache,
    page_table,
    cache_lengths,
    out_weight,
    norm_gain,
    gate_weight,
    up_weight,
    down_weight,
):
    token_position = queries.shape[0]
    group_ratio = QUERY_HEADS // KEY_VALUE_HEADS
    scale = HEAD_SIZE ** (-0.5)
    seq_len = token_position * lax.axis_size("mlp") // REQ_DEV
    place = lax.axis_index("mlp")
    first = place * token_position
    request = first // seq_len
    length = lax.dynamic_index_in_dim(cache_lengths, request, 0, keepdims=False)
    table_row = lax.dynamic_index_in_dim(page_table, request, 0, keepdims=False)
    heads_of_queries = queries.reshape(token_position, KEY_VALUE_HEADS, group_ratio, HEAD_SIZE)

    def update(state, joined_keys, joined_values, valid):
        peak, total, summed = state
        heads_of_keys = joined_keys.reshape(-1, KEY_VALUE_HEADS, HEAD_SIZE)
        heads_of_values = joined_values.reshape(-1, KEY_VALUE_HEADS, HEAD_SIZE)
        scores = (
            jnp.einsum(
                "tgrd,kgd->grtk",
                heads_of_queries,
                heads_of_keys,
                preferred_element_type=jnp.float32,
            )
            * scale
        )
        scores = jnp.where(valid, scores, -1e30)
        new_peak = jnp.maximum(peak, jnp.max(scores, axis=-1))
        expo = jnp.where(valid, jnp.exp(scores - new_peak[..., None]), 0.0)
        factor = jnp.exp(peak - new_peak)
        total = total * factor + jnp.sum(expo, axis=-1)
        summed = summed * factor[..., None] + jnp.einsum(
            "grtk,kgd->grtd",
            expo.astype(jnp.bfloat16),
            heads_of_values,
            preferred_element_type=jnp.float32,
        )
        return (new_peak, total, summed)

    state = (
        jnp.full((KEY_VALUE_HEADS, group_ratio, token_position), -1e30, jnp.float32),
        jnp.zeros((KEY_VALUE_HEADS, group_ratio, token_position), jnp.float32),
        jnp.zeros((KEY_VALUE_HEADS, group_ratio, token_position, HEAD_SIZE), jnp.float32),
    )
    rows_of_queries = first + jnp.arange(token_position, dtype=jnp.int32)
    rows_of_keys = lax.all_gather(fresh_keys, "mlp", axis=0, tiled=True)
    rows_of_values = lax.all_gather(fresh_values, "mlp", axis=0, tiled=True)
    count = rows_of_keys.shape[0]
    key_index = jnp.arange(count, dtype=jnp.int32)
    same = key_index[None, :] // seq_len == rows_of_queries[:, None] // seq_len
    valid = same & (key_index[None, :] <= rows_of_queries[:, None])
    state = update(state, rows_of_keys, rows_of_values, valid)
    key_page = lax.all_gather(paged_key_cache, "mlp", axis=0, tiled=True)
    value_page = lax.all_gather(paged_value_cache, "mlp", axis=0, tiled=True)
    count = key_page.shape[0]
    depth = key_page.shape[1]
    cache_positions = jnp.arange(count, dtype=jnp.int32)
    match = table_row[None, :] == cache_positions[:, None]
    owned = jnp.any(match, axis=1)
    page = jnp.sum(
        jnp.where(match, jnp.arange(table_row.shape[0], dtype=jnp.int32)[None, :], 0), axis=1
    )
    positions = page[:, None] * depth + jnp.arange(depth, dtype=jnp.int32)[None, :]
    live = (owned[:, None] & (positions < length)).reshape(1, count * depth)
    joined_keys = key_page.reshape(count * depth, -1)
    joined_values = value_page.reshape(count * depth, -1)
    state = update(state, joined_keys, joined_values, live)
    peak, total, summed = state
    attended = summed / total[..., None]
    attn = (
        jnp.transpose(attended, (2, 0, 1, 3))
        .reshape(token_position, QUERY_HEADS * HEAD_SIZE)
        .astype(jnp.bfloat16)
    )
    h = resid.astype(jnp.float32) + jnp.dot(attn, out_weight, preferred_element_type=jnp.float32)
    normed = (h * lax.rsqrt(jnp.mean(h * h, axis=-1, keepdims=True) + 1e-05) * norm_gain).astype(
        jnp.bfloat16
    )
    whole = lax.all_gather(normed, "mlp", axis=0, tiled=True)

    def add_rows(piece):
        return jnp.dot(whole, piece, preferred_element_type=jnp.float32)

    gate = add_rows(lax.all_gather(gate_weight, "req", axis=0, tiled=True))
    upper = add_rows(lax.all_gather(up_weight, "req", axis=0, tiled=True))
    hidden = (jax.nn.silu(gate) * upper).astype(jnp.bfloat16)
    terms = jnp.dot(
        hidden,
        lax.all_gather(down_weight, "req", axis=1, tiled=True),
        preferred_element_type=jnp.float32,
    )
    mixed = lax.psum_scatter(
        terms.astype(jnp.bfloat16), "mlp", scatter_dimension=0, tiled=True
    ).astype(jnp.float32)
    return (h + mixed).astype(jnp.bfloat16)


def solution(mesh):
    placed = (
        P(("req", "mlp"), None),
        P(("req", "mlp"), None),
        P(("req", "mlp"), None),
        P(("req", "mlp"), None),
        P(("req", "mlp"), None, None),
        P(("req", "mlp"), None, None),
        P("req", None),
        P("req"),
        P(),
        P(),
        P("req", "mlp"),
        P("req", "mlp"),
        P("mlp", "req"),
    )
    return jax.shard_map(
        body, mesh=mesh, in_specs=placed, out_specs=P(("req", "mlp"), None), check_vma=False
    )
```

profile of v0, /device:TPU:0, one launch (start us, length us, event | category | flops | bytes accessed | tf_op | source)
XLA Modules:
  0.0 476.9 jit_solution(3383910963019407040)
XLA Ops:
  9.4 1.2 copy.43
  11.6 34.4 %all_gather.25 = bf16[1024,256]{1,0:T(8,128)(2,1)S(1)} all-gather(bf16[128,256]{1,0:T(8,128)(2,1)} %param.16), channel_id=1, replica_groups=mesh['req'=4,'mlp'=8] {'mlp'}, dimensions={0}, use_global_device_ids=true | all-gather | bytes 589824 | tf_op jit(solution)/shard_map/all_gather | solution.py:71
  46.0 1.0 copy.46
  48.9 28.2 %all_gather.24 = bf16[1024,256]{0,1:T(8,128)(2,1)S(1)} all-gather(bf16[128,256]{0,1:T(8,128)(2,1)S(1)} %copy.42), channel_id=1, replica_groups=mesh['req'=4,'mlp'=8] {'mlp'}, dimensions={0}, use_global_device_ids=true | all-gather | bytes 589824 | tf_op jit(solution)/shard_map/all_gather | solution.py:70
  77.1 3.8 fusion.8
  80.9 1.4 reshape.148
  82.4 14.6 %all-gather.9.cloned.1.call-done = bf16[16,128,256]{2,1,0:T(8,128)(2,1)} async-done(((bf16[2,128,256]{2,1,0:T(8,128)(2,1)}), bf16[16,128,256]{2,1,0:T(8,128)(2,1)}) %all-gather.9.cloned.1.call-update) | async-done | bytes 1048592 | tf_op jit(solution)/shard_map/all_gather | solution.py:78
  97.0 2.4 reshape.149
  99.3 1.9 bitcast_reduce_fusion
  101.5 1.5 fusion.9
  103.1 3.8 fusion.2
  106.9 1.7 fusion.26
  108.6 3.4 fusion.37
  112.1 1.6 multiply_reduce_fusion
  113.6 1.1 multiply_convert_fusion.1
  116.0 27.7 %all-gather.13.cloned.1.call-done = bf16[3072,1024]{1,0:T(8,128)(2,1)} async-done(((bf16[768,1024]{1,0:T(8,128)(2,1)}), bf16[3072,1024]{1,0:T(8,128)(2,1)}) %all-gather.13.cloned.1.call-update) | async-done | bytes 6291472 | tf_op jit(solution)/shard_map/all_gather | solution.py:108
  143.7 101.1 %all-gather.11.cloned.1.call-done = bf16[1024,3072]{1,0:T(8,128)(2,1)} async-done(((bf16[128,3072]{1,0:T(8,128)(2,1)}), bf16[1024,3072]{1,0:T(8,128)(2,1)}) %all-gather.11.cloned.1.call-update) | async-done | bytes 6291472 | tf_op jit(solution)/shard_map/all_gather | solution.py:103
  244.8 11.9 %fusion.61 = f32[1024,1024]{1,0:T(8,128)} fusion(bf16[1024,3072]{1,0:T(8,128)(2,1)} %all-gather.11.cloned.1.call-done, bf16[3072,1024]{1,0:T(8,128)(2,1)} %all-gather.13.cloned.1.call-done), kind=kOutput, calls=%fused_computation.71 | convolution fusion | flops 6442450944 | bytes 16777216 | tf_op jit(solution)/shard_map/dot_general | solution.py:106
  256.8 34.1 %all-gather.15.cloned.1.call-done = bf16[3072,1024]{1,0:T(8,128)(2,1)} async-done(((bf16[768,1024]{1,0:T(8,128)(2,1)}), bf16[3072,1024]{1,0:T(8,128)(2,1)}) %all-gather.15.cloned.1.call-update) | async-done | bytes 6291472 | tf_op jit(solution)/shard_map/all_gather | solution.py:109
  290.8 12.7 %multiply_convert_fusion = bf16[1024,1024]{1,0:T(8,128)(2,1)} fusion(f32[1024,1024]{1,0:T(8,128)} %fusion.61, bf16[1024,3072]{1,0:T(8,128)(2,1)} %all-gather.11.cloned.1.call-done, bf16[3072,1024]{1,0:T(8,128)(2,1)} %all-gather.15.cloned.1.call-done), kind=kOutput, calls=%fused_computation.16 | convolution fusion | flops 6448742400 | bytes 18874368 | tf_op jit(solution)/shard_map/dot_general | solution.py:106
  303.5 35.1 %all-gather.17.cloned.1.call-done = bf16[1024,3072]{1,0:T(8,128)(2,1)} async-done(((bf16[1024,768]{1,0:T(8,128)(2,1)}), bf16[1024,3072]{1,0:T(8,128)(2,1)}) %all-gather.17.cloned.1.call-update) | async-done | bytes 6291472 | tf_op jit(solution)/shard_map/all_gather | solution.py:113
  338.7 11.1 %convolution_convert_fusion = bf16[1024,3072]{1,0:T(8,128)(2,1)} fusion(bf16[1024,1024]{1,0:T(8,128)(2,1)} %multiply_convert_fusion, bf16[1024,3072]{1,0:T(8,128)(2,1)} %all-gather.17.cloned.1.call-done), kind=kOutput, calls=%fused_computation.12 | convolution fusion | flops 6445596672 | bytes 14680064 | tf_op jit(solution)/shard_map/dot_general | solution.py:111
  349.8 118.1 %reduce-scatter.2.cloned.1.call-done = bf16[128,3072]{1,0:T(8,128)(2,1)} async-done(((bf16[1024,3072]{1,0:T(8,128)(2,1)}), bf16[128,3072]{1,0:T(8,128)(2,1)}) %reduce-scatter.2.cloned.1.call-update) | async-done | bytes 786448 | tf_op jit(solution)/shard_map/reduce_scatter | solution.py:116
  467.8 2.2 add_convert_fusion
  (50 shorter events, 6.5 us)
Async XLA Ops:
  6.5 74.4 %all-gather.7.cloned.1.call-start = ((), (), s32[]{:S(2)}) async-start(), calls=%async_computation.1 | async-start | bytes 1179648 | tf_op jit(solution)/shard_map/all_gather | solution.py:77
  7.3 89.7 %all-gather.9.cloned.1.call-start = ((), (), s32[]{:S(2)}) async-start(), calls=%async_computation.2 | async-start | bytes 1179648 | tf_op jit(solution)/shard_map/all_gather | solution.py:78
  8.0 135.7 %all-gather.13.cloned.1.call-start = ((), (), s32[]{:S(2)}) async-start(), calls=%async_computation.4 | async-start | bytes 7864320 | tf_op jit(solution)/shard_map/all_gather | solution.py:108
  8.7 236.1 %all-gather.11.cloned.1.call-start = ((), (), s32[]{:S(2)}) async-start(), calls=%async_computation.3 | async-start | bytes 7077888 | tf_op jit(solution)/shard_map/all_gather | solution.py:103
  48.9 28.2 %copy-start = (pred[128,1024]{0,1:T(8,128)(4,1)}, pred[128,1024]{0,1:T(8,128)(4,1)S(1)}, u32[]{:S(2)}) copy-start(pred[128,1024]{0,1:T(8,128)(4,1)S(1)} %fusion.42) | copy-start | bytes 393220
  97.0 4.3 slice-start
  99.3 2.2 slice-start.1
  99.3 2.2 copy-start.1
  103.0 3.8 copy-start.4
  106.9 1.7 copy-start.2
  106.9 5.1 %slice-start.2 = ((s8[9437184]{0:T(1024)(128)(4,1)}), s8[4194304]{0:T(1024)(128)(4,1)S(1)}, s32[]{:S(2)}) async-start(s8[9437184]{0:T(1024)(128)(4,1)} %bitcast.105), calls=%async_computation.10 | async-start | bytes 8388608
  108.6 3.4 slice-start.3
  108.6 3.4 slice-start.4
  108.6 3.4 copy-start.3
  112.0 1.6 copy-start.5
  114.8 176.0 %all-gather.15.cloned.1.call-start = ((), (), s32[]{:S(2)}) async-start(), calls=%async_computation.5 | async-start | bytes 7864320 | tf_op jit(solution)/shard_map/all_gather | solution.py:109
  115.4 223.3 %all-gather.17.cloned.1.call-start = ((), (), s32[]{:S(2)}) async-start(), calls=%async_computation.6 | async-start | bytes 7864320 | tf_op jit(solution)/shard_map/all_gather | solution.py:113
  115.9 351.9 %reduce-scatter.2.cloned.1.call-start = ((), (), s32[]{:S(2)}) async-start(), calls=%async_computation.7 | async-start | bytes 7077888 | tf_op jit(solution)/shard_map/reduce_scatter | solution.py:116
Sparse Core Ops, SparseCore 0:
  9.5 44.9 all-gather.6
  56.6 40.3 all-gather.8
  98.5 45.1 all-gather.12
  145.7 99.0 all-gather.10
  246.2 44.5 all-gather.14
  292.2 46.3 all-gather.16
  349.9 117.9 reduce-scatter.1
where the time goes:
time: 477 us
  waiting for transfers between devices  334 us (70%)
  blocking collectives  62.6 us (13%)
  matrix products  48.1 us (10%)
  between operations  14.4 us (3%)
  other arithmetic  10.4 us (2%)
  local copies, waits for them, and re-layouts  7.24 us (2%)
    reduce_scatter x1, waiting for transfers between devices, body(): lax.psum_scatter(terms.astype(jnp.bfloat16), 'mlp', scatter_dimension=0,...  118 us
    all_gather x1, waiting for transfers between devices, body(): whole = lax.all_gather(normed, 'mlp', axis=0, tiled=True)  101 us
    all_gather x1, waiting for transfers between devices, body(): lax.all_gather(down_weight, 'req', axis=1, tiled=True)  35.1 us
    all_gather x1, blocking collectives, body(): rows_of_values = lax.all_gather(fresh_values, 'mlp', axis=0, tiled=True)  34.4 us
    all_gather x1, waiting for transfers between devices, body(): upper = add_rows(lax.all_gather(up_weight, 'req', axis=0, tiled=True))  34.1 us
    all_gather x1, blocking collectives, body(): rows_of_keys = lax.all_gather(fresh_keys, 'mlp', axis=0, tiled=True)  28.2 us
    all_gather x1, waiting for transfers between devices, body(): gate = add_rows(lax.all_gather(gate_weight, 'req', axis=0, tiled=True))  27.7 us
    dot_general x2, matrix products, add_rows(): return jnp.dot(whole, piece, preferred_element_type=jnp.float32)  24.7 us
  transfers between devices with their start and end apart: 7, of which 6 were waited for; matrix products, arithmetic and copies ran while one was open for 11% of the time, Pallas kernels for 0%

commit v1 on v0

--- a/solution.py
+++ b/solution.py
@@ -7,6 +7,25 @@
 KEY_VALUE_HEADS = 2
 HEAD_SIZE = 128
 REQ_DEV = 1
+
+
+def apply_layers_all_in(payload):
+    chip_axis = "req"
+    chips = jax.lax.axis_size(chip_axis)
+    lanes = [(ix, (ix + 1) % chips) for ix in range(chips)]
+    gallery = [(ix, (ix - 1) % chips) for ix in range(chips)]
+    fresh, z1 = ([payload], [payload])
+    for _ in range(chips // 2):
+        fresh.append(jax.lax.ppermute(fresh[-1], chip_axis, lanes))
+    jj = 0
+    while jj < (chips - 1) // 2:
+        z1.append(jax.lax.ppermute(z1[-1], chip_axis, gallery))
+        jj = jj + 1
+    return jnp.roll(
+        jnp.concatenate([*fresh[::-1], *z1[1:]], axis=0),
+        (jax.lax.axis_index(chip_axis) - chips // 2) * payload.shape[0],
+        axis=0,
+    )
 
 
 def body(
@@ -106,7 +125,7 @@
         return jnp.dot(whole, piece, preferred_element_type=jnp.float32)
 
     gate = add_rows(lax.all_gather(gate_weight, "req", axis=0, tiled=True))
-    upper = add_rows(lax.all_gather(up_weight, "req", axis=0, tiled=True))
+    upper = add_rows(apply_layers_all_in(up_weight))
     hidden = (jax.nn.silu(gate) * upper).astype(jnp.bfloat16)
     terms = jnp.dot(
         hidden,

time: 477 us -> 442 us (0.927)
  waiting for transfers between devices: 334 us -> 281 us
  local copies, waits for them, and re-layouts: 7.24 us -> 25.9 us
    ppermute x0 -> x3, waiting for transfers between devices: none -> 78.4 us  [the longest x2 78.4 us: apply_layers_all_in(): fresh.append(jax.lax.ppermute(fresh[-1], chip_axis, lanes))]
    all_gather x1, waiting for transfers between devices: 101 us -> 43 us  [body(): whole = lax.all_gather(normed, 'mlp', axis=0, tiled=True)]
    all_gather x1 -> x0, waiting for transfers between devices: 34.1 us -> none  [body(): upper = add_rows(lax.all_gather(up_weight, 'req', axis=0, tiled=True))]
    all_gather x1, waiting for transfers between devices: 27.7 us -> 0.01 us  [body(): gate = add_rows(lax.all_gather(gate_weight, 'req', axis=0, tiled=True))]
    unnamed x24 -> x35, local copies, waits for them, and re-layouts: 2.44 us -> 18.5 us
    all_gather x1, waiting for transfers between devices: 35.1 us -> 24.4 us  [body(): lax.all_gather(down_weight, 'req', axis=1, tiled=True)]
  transfers between devices with their start and end apart: 7 -> 9, of which waited for: 6 -> 6; matrix products, arithmetic and copies ran while one was open for 11% -> 15% of each run, Pallas kernels for 0% -> 0%
where the time goes in v1:
time: 442 us; the launch traced here: 441 us
  waiting for transfers between devices  281 us (64%)
  blocking collectives  62.5 us (14%)
  matrix products  45.2 us (10%)
  local copies, waits for them, and re-layouts  25.9 us (6%)
  between operations  14.4 us (3%)
  other arithmetic  10.4 us (2%)
    reduce_scatter x1, waiting for transfers between devices, body(): lax.psum_scatter(terms.astype(jnp.bfloat16), 'mlp', scatter_dimension=0,...  118 us
    ppermute x2, waiting for transfers between devices, apply_layers_all_in(): fresh.append(jax.lax.ppermute(fresh[-1], chip_axis, lanes))  78.4 us
    all_gather x1, waiting for transfers between devices, body(): whole = lax.all_gather(normed, 'mlp', axis=0, tiled=True)  43 us
    all_gather x1, blocking collectives, body(): rows_of_values = lax.all_gather(fresh_values, 'mlp', axis=0, tiled=True)  34.4 us
    all_gather x1, blocking collectives, body(): rows_of_keys = lax.all_gather(fresh_keys, 'mlp', axis=0, tiled=True)  28.1 us
    all_gather x1, waiting for transfers between devices, body(): lax.all_gather(down_weight, 'req', axis=1, tiled=True)  24.4 us
    dot_general x2, matrix products, add_rows(): return jnp.dot(whole, piece, preferred_element_type=jnp.float32)  21.6 us
    unnamed x35, local copies, waits for them, and re-layouts  18.5 us
  transfers between devices with their start and end apart: 9, of which 6 were waited for; matrix products, arithmetic and copies ran while one was open for 15% of the time, Pallas kernels for 0%

profile of v1, /device:TPU:0, one launch (start us, length us, event | category | flops | bytes accessed | tf_op | source)
XLA Modules:
  0.0 441.2 jit_solution(1855884260099141964)
XLA Ops:
  11.6 34.4 %all_gather.22 = bf16[1024,256]{1,0:T(8,128)(2,1)S(1)} all-gather(bf16[128,256]{1,0:T(8,128)(2,1)} %param.16), channel_id=1, replica_groups=mesh['req'=4,'mlp'=8] {'mlp'}, dimensions={0}, use_global_device_ids=true | all-gather | bytes 589824 | tf_op jit(solution)/shard_map/all_gather | solution.py:90
  48.9 28.1 %all_gather.21 = bf16[1024,256]{0,1:T(8,128)(2,1)S(1)} all-gather(bf16[128,256]{0,1:T(8,128)(2,1)S(1)} %copy.42), channel_id=1, replica_groups=mesh['req'=4,'mlp'=8] {'mlp'}, dimensions={0}, use_global_device_ids=true | all-gather | bytes 589824 | tf_op jit(solution)/shard_map/all_gather | solution.py:89
  77.0 3.8 fusion.10
  82.1 14.2 %all-gather.8.cloned.1.call-done = bf16[16,128,256]{2,1,0:T(8,128)(2,1)} async-done(((bf16[2,128,256]{2,1,0:T(8,128)(2,1)}), bf16[16,128,256]{2,1,0:T(8,128)(2,1)}) %all-gather.8.cloned.1.call-update) | async-done | bytes 1048592 | tf_op jit(solution)/shard_map/all_gather | solution.py:97
  96.3 2.4 reshape.149
  98.7 1.9 bitcast_reduce_fusion
  102.4 3.8 fusion.2
  108.0 3.4 fusion.41
  114.9 43.5 %collective-permute-done = bf16[768,1024]{1,0:T(8,128)(2,1)} collective-permute-done((bf16[768,1024]{1,0:T(8,128)(2,1)S(1)}, bf16[768,1024]{1,0:T(8,128)(2,1)}, u32[]{:S(2)}, u32[]{:S(2)}) %collective-permute-start) | collective-permute-done | bytes 1572896 | tf_op jit(solution)/shard_map/ppermute | solution.py:19
  158.3 1.7 collective-permute-start.2
  160.1 34.9 %collective-permute-done.1 = bf16[768,1024]{1,0:T(8,128)(2,1)} collective-permute-done((bf16[768,1024]{1,0:T(8,128)(2,1)}, bf16[768,1024]{1,0:T(8,128)(2,1)}, u32[]{:S(2)}, u32[]{:S(2)}) %collective-permute-start.1) | collective-permute-done | bytes 1572896 | tf_op jit(solution)/shard_map/ppermute | solution.py:19
  195.0 2.7 constant_dynamic-update-slice_fusion.7
  197.7 2.7 constant_dynamic-update-slice_fusion.6
  201.6 2.7 constant_dynamic-update-slice_fusion.4
  204.4 2.7 constant_dynamic-update-slice_fusion.3
  207.0 2.8 constant_dynamic-update-slice_fusion.2
  211.1 2.7 constant_dynamic-update-slice_fusion
  213.8 43.0 %all-gather.10.cloned.1.call-done = bf16[1024,3072]{1,0:T(8,128)(2,1)} async-done(((bf16[128,3072]{1,0:T(8,128)(2,1)}), bf16[1024,3072]{1,0:T(8,128)(2,1)}) %all-gather.10.cloned.1.call-update) | async-done | bytes 6291472 | tf_op jit(solution)/shard_map/all_gather | solution.py:122
  256.8 11.3 %fusion.66 = f32[1024,1024]{1,0:T(8,128)S(1)} fusion(bf16[1024,3072]{1,0:T(8,128)(2,1)} %all-gather.10.cloned.1.call-done, bf16[3072,1024]{1,0:T(8,128)(2,1)} %all-gather.12.cloned.1.call-done), kind=kOutput, calls=%fused_computation.82 | convolution fusion | flops 6442450944 | bytes 16777216 | tf_op jit(solution)/shard_map/dot_general | solution.py:125
  268.1 10.3 %multiply_convert_fusion = bf16[1024,1024]{1,0:T(8,128)(2,1)} fusion(f32[1024,1024]{1,0:T(8,128)S(1)} %fusion.66, bf16[1024,3072]{1,0:T(8,128)(2,1)S(1)} %copy-done.7, bf16[6144,1024]{1,0:T(8,128)(2,1)} %constant_dynamic-update-slice_fusion, s32[]{:T(128)S(6)} %select_n.69), kind=kOutput, calls=%fused_computation.18 | convolution fusion | flops 6448742400 | bytes 18874372 | tf_op jit(solution)/shard_map/dot_general | solution.py:125
  278.4 24.4 %all-gather.14.cloned.1.call-done = bf16[1024,3072]{1,0:T(8,128)(2,1)} async-done(((bf16[1024,768]{1,0:T(8,128)(2,1)}), bf16[1024,3072]{1,0:T(8,128)(2,1)}) %all-gather.14.cloned.1.call-update) | async-done | bytes 6291472 | tf_op jit(solution)/shard_map/all_gather | solution.py:132
  302.8 11.2 %convolution_convert_fusion = bf16[1024,3072]{1,0:T(8,128)(2,1)} fusion(bf16[1024,1024]{1,0:T(8,128)(2,1)} %multiply_convert_fusion, bf16[1024,3072]{1,0:T(8,128)(2,1)} %all-gather.14.cloned.1.call-done), kind=kOutput, calls=%fused_computation.14 | convolution fusion | flops 6445596672 | bytes 14680064 | tf_op jit(solution)/shard_map/dot_general | solution.py:130
  314.0 118.1 %reduce-scatter.2.cloned.1.call-done = bf16[128,3072]{1,0:T(8,128)(2,1)} async-done(((bf16[1024,3072]{1,0:T(8,128)(2,1)}), bf16[128,3072]{1,0:T(8,128)(2,1)}) %reduce-scatter.2.cloned.1.call-update) | async-done | bytes 786448 | tf_op jit(solution)/shard_map/reduce_scatter | solution.py:135
  432.2 2.2 add_convert_fusion
  (65 shorter events, 18.0 us)
Async XLA Ops:
  6.5 74.2 %all-gather.6.cloned.1.call-start = ((), (), s32[]{:S(2)}) async-start(), calls=%async_computation.1 | async-start | bytes 1179648 | tf_op jit(solution)/shard_map/all_gather | solution.py:96
  7.3 89.1 %all-gather.8.cloned.1.call-start = ((), (), s32[]{:S(2)}) async-start(), calls=%async_computation.2 | async-start | bytes 1179648 | tf_op jit(solution)/shard_map/all_gather | solution.py:97
  8.0 205.8 %all-gather.12.cloned.1.call-start = ((), (), s32[]{:S(2)}) async-start(), calls=%async_computation.4 | async-start | bytes 7864320 | tf_op jit(solution)/shard_map/all_gather | solution.py:127
  8.7 248.0 %all-gather.10.cloned.1.call-start = ((), (), s32[]{:S(2)}) async-start(), calls=%async_computation.3 | async-start | bytes 7077888 | tf_op jit(solution)/shard_map/all_gather | solution.py:122
  48.9 28.1 %copy-start.1 = (pred[128,1024]{0,1:T(8,128)(4,1)}, pred[128,1024]{0,1:T(8,128)(4,1)S(1)}, u32[]{:S(2)}) copy-start(pred[128,1024]{0,1:T(8,128)(4,1)S(1)} %fusion.46) | copy-start | bytes 393220
  96.3 4.3 slice-start
  98.7 2.2 slice-start.1
  98.7 2.2 copy-start.2
  102.4 3.8 copy-start.5
  106.2 1.7 copy-start.3
  106.2 5.1 %slice-start.2 = ((s8[9437184]{0:T(1024)(128)(4,1)}), s8[4194304]{0:T(1024)(128)(4,1)S(1)}, s32[]{:S(2)}) async-start(s8[9437184]{0:T(1024)(128)(4,1)} %bitcast.104), calls=%async_computation.9 | async-start | bytes 8388608
  107.9 3.4 slice-start.3
  107.9 3.4 slice-start.4
  108.0 3.4 copy-start.4
  111.4 1.6 copy-start.6
  111.4 3.4 copy-start
  114.1 188.6 %all-gather.14.cloned.1.call-start = ((), (), s32[]{:S(2)}) async-start(), calls=%async_computation.5 | async-start | bytes 7864320 | tf_op jit(solution)/shard_map/all_gather | solution.py:132
  114.7 317.4 %reduce-scatter.2.cloned.1.call-start = ((), (), s32[]{:S(2)}) async-start(), calls=%async_computation.6 | async-start | bytes 7077888 | tf_op jit(solution)/shard_map/reduce_scatter | solution.py:135
  114.8 43.5 %collective-permute-start = (bf16[768,1024]{1,0:T(8,128)(2,1)S(1)}, bf16[768,1024]{1,0:T(8,128)(2,1)}, u32[]{:S(2)}, u32[]{:S(2)}) collective-permute-start(bf16[768,1024]{1,0:T(8,128)(2,1)S(1)} %copy-done), channel_id=1, source_target_pairs={{0,8},{8,16},{16,24},{24,0},{1,9},{9,17},{17,25},{25,1},{2,10},{10... | collective-permute-start | bytes 4718600 | tf_op jit(solution)/shard_map/ppermute | solution.py:19
  158.3 36.7 %collective-permute-start.1 = (bf16[768,1024]{1,0:T(8,128)(2,1)}, bf16[768,1024]{1,0:T(8,128)(2,1)}, u32[]{:S(2)}, u32[]{:S(2)}) collective-permute-start(bf16[768,1024]{1,0:T(8,128)(2,1)} %collective-permute-done), channel_id=1, source_target_pairs={{0,8},{8,16},{16,24},{24,0},{1,9},{9,17},{17,25},{25,1},{2,10},{10... | collective-permute-start | bytes 4718600 | tf_op jit(solution)/shard_map/ppermute | solution.py:19
  158.3 43.3 %collective-permute-start.2 = (bf16[768,1024]{1,0:T(8,128)(2,1)S(1)}, bf16[768,1024]{1,0:T(8,128)(2,1)}, u32[]{:S(2)}, u32[]{:S(2)}) collective-permute-start(bf16[768,1024]{1,0:T(8,128)(2,1)S(1)} %copy-done), channel_id=1, source_target_pairs={{0,24},{8,0},{16,8},{24,16},{1,25},{9,1},{17,9},{25,17},{2,26},{10... | collective-permute-start | bytes 4718600 | tf_op jit(solution)/shard_map/ppermute | solution.py:22
  256.8 11.3 %copy-start.7 = (bf16[1024,3072]{1,0:T(8,128)(2,1)S(1)}, bf16[1024,3072]{1,0:T(8,128)(2,1)}, u32[]{:S(2)}) copy-start(bf16[1024,3072]{1,0:T(8,128)(2,1)} %all-gather.10.cloned.1.call-done) | copy-start | bytes 18874372
Sparse Core Ops, SparseCore 0:
  9.5 45.0 all-gather.5
  56.7 39.6 all-gather.7
  97.9 57.0 all-gather.11
  157.0 99.7 all-gather.9
  258.2 44.5 all-gather.13
  314.1 117.9 reduce-scatter.1
